TPU v7x, 32 devices: a whole 2x2x4 slice. The times are simulated.
32 devices in a mesh: rep: 4 (over y, x), shard: 2 (over core), exp: 4 (over z).
Axes of the slice: x: 2, y: 2, z: 4, core: 2. Of those that a mesh axis runs over, the one named last changes fastest.
Arguments:
- tokens: bfloat16 [2048, 2560], P(('rep', 'exp')), may hold values from -6 to 6
- expert_of: int32 [2048, 1], P(('rep', 'exp')), may hold values from 0 to 3; in each aligned block of 128 rows (0 to 127, 128 to 255, ...) at most 80 rows name the same one
- w_gate: bfloat16 [4, 768, 2560], P('exp', 'shard'), may hold values from -0.125 to 0.125
- w_up: bfloat16 [4, 768, 2560], P('exp', 'shard'), may hold values from -0.125 to 0.125
- d_hidden: bfloat16 [4, 4, 4, 80, 768], P('rep', 'exp', None, None, 'shard'), may hold values from -6 to 6
Outputs:
- hidden: bfloat16 [4, 4, 4, 80, 768], P('rep', 'exp', None, None, 'shard')
- d_tokens: bfloat16 [2048, 2560], P(('rep', 'exp'), 'shard')
- grad_gate: bfloat16 [4, 768, 2560], P('exp', 'shard')
- grad_up: bfloat16 [4, 768, 2560], P('exp', 'shard')
Inputs may be any that keep to these rules, and one draw needn't show every extreme that they name: `expert_of`: each value names an expert. Among the 128 tokens of one device (aligned blocks of rows), no expert is named more than 80 times, a bound that some block reaches.
All inputs are finite; a program needn't handle non-finite values.
Results may differ from a plain program's by a relative error of at most 0.017.
Values may be sent and summed in bfloat16 or wider, within the bound.
No kernel may reach another device: no remote copies, remote signals or barrier semaphores. Data moves between devices by JAX's collectives and lax.ppermute only.
A program may use at most 64 MiB of HBM per device.

v0:
```python
import jax
import jax.numpy as jnp
from jax import lax
from jax.sharding import PartitionSpec as P


def local(tokens, expert_of, w_gate, w_up, d_hidden):
    expert_count = lax.axis_size("exp")
    replica_count = lax.axis_size("rep")
    capacity = d_hidden.shape[3]
    feature_width = tokens.shape[1]
    slots_all = expert_count * capacity
    routed = expert_of[:, 0]
    chosen = (routed[:, None] == jnp.arange(expert_count, dtype=jnp.int32)[None, :]).astype(
        jnp.int32
    )
    slot_index = jnp.sum(chosen * (jnp.cumsum(chosen, axis=0) - 1), axis=1)
    target = routed * capacity + slot_index
    placing = (jnp.arange(slots_all, dtype=jnp.int32)[:, None] == target[None, :]).astype(
        jnp.bfloat16
    )
    packed = jnp.dot(placing, tokens, preferred_element_type=jnp.float32).astype(jnp.bfloat16)
    arrived = lax.all_to_all(
        packed.reshape(expert_count, capacity, feature_width),
        "exp",
        split_axis=0,
        concat_axis=0,
        tiled=True,
    )
    expert_rows = arrived.reshape(slots_all, feature_width)
    gate_rows = w_gate[0]
    up_rows = w_up[0]
    contract_last = (((1,), (1,)), ((), ()))
    gate_act = lax.dot_general(
        expert_rows, gate_rows, contract_last, preferred_element_type=jnp.float32
    )
    up_act = lax.dot_general(
        expert_rows, up_rows, contract_last, preferred_element_type=jnp.float32
    )
    sigma = jax.nn.sigmoid(gate_act)
    hidden = (gate_act * sigma * up_act).astype(jnp.bfloat16)
    cotan = d_hidden.reshape(slots_all, gate_rows.shape[0]).astype(jnp.float32)
    grad_gate_act = (cotan * up_act * sigma * (1.0 + gate_act * (1.0 - sigma))).astype(jnp.bfloat16)
    grad_up_act = (cotan * gate_act * sigma).astype(jnp.bfloat16)
    contract_first = (((0,), (0,)), ((), ()))
    part_gate = lax.dot_general(
        grad_gate_act, expert_rows, contract_first, preferred_element_type=jnp.float32
    )
    part_up = lax.dot_general(
        grad_up_act, expert_rows, contract_first, preferred_element_type=jnp.float32
    )
    total_gate, total_up = (
        lax.psum(
            part_gate.astype(jnp.bfloat16).astype(jnp.float32).astype(jnp.bfloat16), "rep"
        ).astype(jnp.float32),
        lax.psum(
            part_up.astype(jnp.bfloat16).astype(jnp.float32).astype(jnp.bfloat16), "rep"
        ).astype(jnp.float32),
    )
    grad_gate = (total_gate * (1.0 / replica_count)).astype(jnp.bfloat16)[None]
    grad_up = (total_up * (1.0 / replica_count)).astype(jnp.bfloat16)[None]
    partial_value = jnp.dot(grad_gate_act, gate_rows, preferred_element_type=jnp.float32)
    partial_value = partial_value + jnp.dot(
        grad_up_act, up_rows, preferred_element_type=jnp.float32
    )
    outgoing = partial_value.astype(jnp.bfloat16).reshape(expert_count, capacity, feature_width)
    returned = lax.all_to_all(outgoing, "exp", split_axis=0, concat_axis=0, tiled=True)
    unpacked = lax.dot_general(
        placing,
        returned.reshape(slots_all, feature_width),
        contract_first,
        preferred_element_type=jnp.float32,
    )
    d_tokens = lax.psum_scatter(
        unpacked.astype(jnp.bfloat16), "shard", scatter_dimension=1, tiled=True
    )
    return (hidden.reshape(d_hidden.shape), d_tokens, grad_gate, grad_up)


def solution(mesh):
    in_specs = (
        P(("rep", "exp"), None),
        P(("rep", "exp"), None),
        P("exp", "shard", None),
        P("exp", "shard", None),
        P("rep", "exp", None, None, "shard"),
    )
    out_specs = (
        P("rep", "exp", None, None, "shard"),
        P(("rep", "exp"), "shard"),
        P("exp", "shard", None),
        P("exp", "shard", None),
    )
    return jax.shard_map(local, mesh=mesh, in_specs=in_specs, out_specs=out_specs, check_vma=False)
```

profile of v0, /device:TPU:0, one launch (start us, length us, event | category | flops | bytes accessed | tf_op | source)
XLA Modules:
  0.0 176.9 jit_solution(2150093289877161744)
XLA Ops:
  8.0 0.0 copy-start
  8.0 0.0 all-reduce.3.cloned.1.call-start
  8.1 0.9 fusion.17
  8.9 0.2 reduce_window_sum.11
  9.1 0.8 select_reduce_fusion
  9.9 0.7 multiply_add_fusion
  10.6 1.7 convolution_convert_fusion.2
  12.3 0.0 copy-start.1
  12.3 44.6 %all_to_all.10 = bf16[4,80,2560]{2,1,0:T(8,128)(2,1)S(1)} all-to-all(bf16[4,80,2560]{2,1,0:T(8,128)(2,1)S(1)} %bitcast.39), channel_id=1, replica_groups=mesh['rep'=4,'shard'=2,'exp'=4] {'exp'}, dimensions={0} | all-to-all | bytes 3276800 | tf_op jit(solution)/shard_map/all_to_all | solution.py:23
  56.9 0.0 copy-done.1
  56.9 0.0 copy-start.2
  56.9 1.0 fusion.8
  57.9 0.0 copy-done
  57.9 0.0 copy-done.2
  57.9 1.9 %fusion.12 = (bf16[320,384]{1,0:T(8,128)(2,1)S(1)}, bf16[320,384]{1,0:T(8,128)(2,1)}, bf16[320,384]{1,0:T(8,128)(2,1)S(1)}) fusion(f32[320,384]{1,0:T(8,128)S(1)} %fusion.8, bf16[1,1,4,80,384]{4,3,2,1,0:T(8,128)(2,1)S(1)} %copy-done.2, bf16[320,2560]{1,0:T(8,128)(2,1)S(1)} %bitcast.41, bf16[1,384,2560]{2,1,0:T(8,128)(2,1)S(1)} %copy-done), kind=kOutput, calls=%fused_computation.21 | convolution fusion | flops 631234560 | bytes 5079040 | tf_op jit(solution)/shard_map/dot_general | solution.py:37
  59.8 2.5 %convolution_convert_fusion.1 = bf16[384,2560]{1,0:T(8,128)(2,1)} fusion(bf16[320,384]{1,0:T(8,128)(2,1)S(1)} %get-tuple-element.6, bf16[320,2560]{1,0:T(8,128)(2,1)S(1)} %bitcast.42), kind=kOutput, calls=%fused_computation.2 | convolution fusion | flops 630128640 | bytes 3850240 | tf_op jit(solution)/shard_map/dot_general | solution.py:46
  62.3 2.5 %convolution_convert_fusion = bf16[384,2560]{1,0:T(8,128)(2,1)} fusion(bf16[320,384]{1,0:T(8,128)(2,1)S(1)} %get-tuple-element.8, bf16[320,2560]{1,0:T(8,128)(2,1)S(1)} %bitcast.43), kind=kOutput, calls=%fused_computation.1 | convolution fusion | flops 630128640 | bytes 3850240 | tf_op jit(solution)/shard_map/dot_general | solution.py:49
  64.8 0.0 all-reduce.3.cloned.1.call-update
  64.8 0.0 reduce-scatter.2.cloned.1.call-start
  64.9 2.6 %fusion.6 = f32[320,2560]{1,0:T(8,128)S(1)} fusion(bf16[320,384]{1,0:T(8,128)(2,1)S(1)} %get-tuple-element.6, bf16[1,384,2560]{2,1,0:T(8,128)(2,1)} %param.7), kind=kOutput, calls=%fused_computation.13 | convolution fusion | flops 629145600 | bytes 5488640 | tf_op jit(solution)/shard_map/dot_general | solution.py:62
  67.4 1.0 fusion
  68.5 40.2 %all_to_all.11 = bf16[4,80,2560]{2,1,0:T(8,128)(2,1)S(1)} all-to-all(bf16[4,80,2560]{2,1,0:T(8,128)(2,1)S(1)} %bitcast.37), channel_id=1, replica_groups=mesh['rep'=4,'shard'=2,'exp'=4] {'exp'}, dimensions={0} | all-to-all | bytes 3276800 | tf_op jit(solution)/shard_map/all_to_all | solution.py:67
  108.7 1.4 convolution_convert_fusion.3
  110.1 0.0 reduce-scatter.2.cloned.1.call-update
  110.1 54.6 %all-reduce.3.cloned.1.call-done = (bf16[384,2560]{1,0:T(8,128)(2,1)}, bf16[384,2560]{1,0:T(8,128)(2,1)}) async-done(((bf16[384,2560]{1,0:T(8,128)(2,1)}, bf16[384,2560]{1,0:T(8,128)(2,1)}), (bf16[384,2560]{1,0:T(8,128)(2,1)}, bf16[384,2560]{1,0:T(8,128)(2,1)})) %all-reduce.3.cloned.1.call-update) | async-done | bytes 3932176 | tf_op jit(solution)/shard_map/psum | solution.py:53
  164.7 4.7 %fusion.1 = (bf16[1,384,2560]{2,1,0:T(8,128)(2,1)}, bf16[1,384,2560]{2,1,0:T(8,128)(2,1)}) fusion(bf16[384,2560]{1,0:T(8,128)(2,1)} %get-tuple-element.4, bf16[384,2560]{1,0:T(8,128)(2,1)} %get-tuple-element.5), kind=kLoop, calls=%fused_computation.8 | loop fusion | flops 5898240 | bytes 7864320 | tf_op jit(solution)/shard_map/broadcast_in_dim | solution.py:60
  169.4 0.0 reduce-scatter.2.cloned.1.call-done
Async XLA Ops:
  8.0 49.9 %copy-start = (bf16[1,384,2560]{2,1,0:T(8,128)(2,1)S(1)}, bf16[1,384,2560]{2,1,0:T(8,128)(2,1)}, u32[]{:S(2)}) copy-start(bf16[1,384,2560]{2,1,0:T(8,128)(2,1)} %param.8) | copy-start | bytes 5898244
  8.0 156.7 %all-reduce.3.cloned.1.call-start = ((), (), s32[]{:S(2)}) async-start(), calls=%async_computation.4 | async-start | bytes 7864320 | tf_op jit(solution)/shard_map/psum | solution.py:53
  12.3 44.6 %copy-start.1 = (bf16[1,384,2560]{2,1,0:T(8,128)(2,1)S(1)}, bf16[1,384,2560]{2,1,0:T(8,128)(2,1)}, u32[]{:S(2)}) copy-start(bf16[1,384,2560]{2,1,0:T(8,128)(2,1)} %param.7) | copy-start | bytes 5898244
  56.9 1.0 copy-start.2
  64.8 104.6 %reduce-scatter.2.cloned.1.call-start = ((), (), s32[]{:S(2)}) async-start(), calls=%async_computation.3 | async-start | bytes 983040 | tf_op jit(solution)/shard_map/reduce_scatter | solution.py:74
Sparse Core Ops, SparseCore 0:
  64.9 99.7 all-reduce.2
Sparse Core Ops, SparseCore 1:
  110.2 7.1 reduce-scatter.1
where the time goes:
time: 177 us
  blocking collectives  84.9 us (48%)
  waiting for transfers between devices  54.6 us (31%)
  between operations  15.5 us (9%)
  matrix products  14.5 us (8%)
  other arithmetic  7.28 us (4%)
    psum x1, waiting for transfers between devices, local(): lax.psum(part_gate.astype(jnp.bfloat16).astype(jnp.float32).astype(jnp.bf...  54.6 us
    all_to_all x1, blocking collectives, local(): lax.all_to_all(packed.reshape(expert_count, capacity, feature_width), 'ex...  44.6 us
    all_to_all x1, blocking collectives, local(): lax.all_to_all(outgoing, 'exp', split_axis=0, concat_axis=0, tiled=True)  40.2 us
    broadcast_in_dim x1, other arithmetic, local(): grad_gate = (total_gate * (1.0 / replica_count)).astype(jnp.bfloat16)[None]  4.75 us
  transfers between devices with their start and end apart: 2, of which 1 were waited for; matrix products, arithmetic and copies ran while one was open for 5% of the time, Pallas kernels for 0%

commit v1 on v0

--- a/solution.py
+++ b/solution.py
@@ -20,13 +20,19 @@
         jnp.bfloat16
     )
     packed = jnp.dot(placing, tokens, preferred_element_type=jnp.float32).astype(jnp.bfloat16)
-    arrived = lax.all_to_all(
-        packed.reshape(expert_count, capacity, feature_width),
-        "exp",
-        split_axis=0,
-        concat_axis=0,
-        tiled=True,
-    )
+    value = packed.reshape(expert_count, capacity, feature_width)
+    ways, here = (lax.axis_size("exp"), lax.axis_index("exp"))
+    width = value.shape[0] // ways
+    shape = list(value.shape)
+    shape[0] = width
+    height = shape[0]
+    shape[0] = height * ways
+    arrived = jnp.zeros(shape, value.dtype)
+    for mask in range(ways):
+        part = lax.dynamic_slice_in_dim(value, (here ^ mask) * width, width, axis=0)
+        if mask:
+            part = lax.ppermute(part, "exp", [(d, d ^ mask) for d in range(ways)])
+        arrived = lax.dynamic_update_slice_in_dim(arrived, part, (here ^ mask) * height, axis=0)
     expert_rows = arrived.reshape(slots_all, feature_width)
     gate_rows = w_gate[0]
     up_rows = w_up[0]

time: 177 us -> 177 us (level)
  blocking collectives: 84.9 us -> 47.2 us
  waiting for transfers between devices: 54.6 us -> 83.2 us
  starting transfers between devices: 0.08 us -> 5.75 us
    all_to_all x1 -> x0, blocking collectives: 44.6 us -> none  [local(): lax.all_to_all(packed.reshape(expert_count, capacity, feature_width), 'ex...]
    ppermute x0 -> x3, waiting for transfers between devices: none -> 28.2 us  [local(): part = lax.ppermute(part, 'exp', [(d, d ^ mask) for d in range(ways)])]
    all_to_all x1, blocking collectives: 40.2 us -> 47.2 us  [local(): lax.all_to_all(outgoing, 'exp', split_axis=0, concat_axis=0, tiled=True)]
    ppermute x0 -> x3, starting transfers between devices: none -> 5.67 us  [local(): part = lax.ppermute(part, 'exp', [(d, d ^ mask) for d in range(ways)])]
  transfers between devices with their start and end apart: 2 -> 5, of which waited for: 1 -> 3; matrix products, arithmetic and copies ran while one was open for 5% -> 6% of each run, Pallas kernels for 0% -> 0%
where the time goes in v1:
time: 177 us; the launch traced here: 176 us
  waiting for transfers between devices  83.2 us (47%)
  blocking collectives  47.2 us (27%)
  matrix products  15.7 us (9%)
  between operations  15.6 us (9%)
  other arithmetic  7.28 us (4%)
  starting transfers between devices  5.75 us (3%)
    psum x1, waiting for transfers between devices, local(): lax.psum(part_gate.astype(jnp.bfloat16).astype(jnp.float32).astype(jnp.bf...  55 us
    all_to_all x1, blocking collectives, local(): lax.all_to_all(outgoing, 'exp', split_axis=0, concat_axis=0, tiled=True)  47.2 us
    ppermute x3, waiting for transfers between devices, local(): part = lax.ppermute(part, 'exp', [(d, d ^ mask) for d in range(ways)])  28.2 us
    ppermute x3, starting transfers between devices, local(): part = lax.ppermute(part, 'exp', [(d, d ^ mask) for d in range(ways)])  5.67 us
    broadcast_in_dim x1, other arithmetic, local(): grad_gate = (total_gate * (1.0 / replica_count)).astype(jnp.bfloat16)[None]  4.75 us
  transfers between devices with their start and end apart: 5, of which 3 were waited for; matrix products, arithmetic and copies ran while one was open for 6% of the time, Pallas kernels for 0%

profile of v1, /device:TPU:0, one launch (start us, length us, event | category | flops | bytes accessed | tf_op | source)
XLA Modules:
  0.0 176.4 jit_solution(16181398130571000451)
XLA Ops:
  8.0 0.0 copy-start
  8.0 0.0 all-reduce.3.cloned.1.call-start
  8.1 0.9 fusion.17
  8.9 0.2 reduce_window_sum.11
  9.1 0.8 select_reduce_fusion
  9.9 0.7 multiply_add_fusion
  10.6 2.8 %convolution_convert_fusion.2 = bf16[320,2560]{1,0:T(8,128)(2,1)} fusion(bf16[128,2560]{1,0:T(8,128)(2,1)} %param.5, s32[128]{0:T(128)S(1)} %multiply_add_fusion), kind=kOutput, calls=%fused_computation.4 | convolution fusion | flops 210575360 | bytes 2294272 | tf_op jit(solution)/shard_map/dot_general | solution.py:22
  13.4 0.0 copy-start.1
  13.4 0.1 broadcast_in_dim.12
  13.6 1.3 copy-done.1
  14.9 0.1 constant_dynamic-slice_fusion.2
  15.0 0.0 copy-start.2
  15.0 3.1 %collective-permute-start = (bf16[1,80,2560]{2,1,0:T(8,128)(2,1)S(1)}, bf16[1,80,2560]{2,1,0:T(8,128)(2,1)S(1)}, u32[]{:S(2)}, u32[]{:S(2)}) collective-permute-start(bf16[1,80,2560]{2,1,0:T(8,128)(2,1)S(1)} %get-tuple-element.8), channel_id=1, source_target_pairs={{0,1},{1,0},{2,3},{3,2},{4,5},{5,4},{6,7},{7,6},{8,9},{9,8},{10,11... | collective-permute-start | bytes 1228808 | tf_op jit(solution)/shard_map/ppermute | solution.py:34
  18.1 2.6 %collective-permute-start.1 = (bf16[1,80,2560]{2,1,0:T(8,128)(2,1)S(1)}, bf16[1,80,2560]{2,1,0:T(8,128)(2,1)S(1)}, u32[]{:S(2)}, u32[]{:S(2)}) collective-permute-start(bf16[1,80,2560]{2,1,0:T(8,128)(2,1)S(1)} %get-tuple-element.7), channel_id=1, source_target_pairs={{0,2},{1,3},{2,0},{3,1},{4,6},{5,7},{6,4},{7,5},{8,10},{9,11},{10,... | collective-permute-start | bytes 1228808 | tf_op jit(solution)/shard_map/ppermute | solution.py:34
  20.7 0.0 collective-permute-start.2
  20.7 14.9 %collective-permute-done = bf16[1,80,2560]{2,1,0:T(8,128)(2,1)S(1)} collective-permute-done((bf16[1,80,2560]{2,1,0:T(8,128)(2,1)S(1)}, bf16[1,80,2560]{2,1,0:T(8,128)(2,1)S(1)}, u32[]{:S(2)}, u32[]{:S(2)}) %collective-permute-start) | collective-permute-done | bytes 409632 | tf_op jit(solution)/shard_map/ppermute | solution.py:34
  35.6 13.3 %collective-permute-done.1 = bf16[1,80,2560]{2,1,0:T(8,128)(2,1)S(1)} collective-permute-done((bf16[1,80,2560]{2,1,0:T(8,128)(2,1)S(1)}, bf16[1,80,2560]{2,1,0:T(8,128)(2,1)S(1)}, u32[]{:S(2)}, u32[]{:S(2)}) %collective-permute-start.1) | collective-permute-done | bytes 409632 | tf_op jit(solution)/shard_map/ppermute | solution.py:34
  49.0 0.0 collective-permute-done.2
  49.0 0.0 copy-done.2
  49.0 0.0 copy-start.3
  49.1 1.0 fusion.8
  50.1 0.0 copy-done
  50.1 0.0 copy-done.3
  50.1 1.9 %fusion.12 = (bf16[320,384]{1,0:T(8,128)(2,1)S(1)}, bf16[320,384]{1,0:T(8,128)(2,1)}, bf16[320,384]{1,0:T(8,128)(2,1)S(1)}) fusion(f32[320,384]{1,0:T(8,128)S(1)} %fusion.8, bf16[1,1,4,80,384]{4,3,2,1,0:T(8,128)(2,1)S(1)} %copy-done.3, bf16[320,2560]{1,0:T(8,128)(2,1)S(1)} %bitcast.41, bf16[1,384,2560]{2,1,0:T(8,128)(2,1)S(1)} %copy-done), kind=kOutput, calls=%fused_computation.21 | convolution fusion | flops 631234560 | bytes 5079040 | tf_op jit(solution)/shard_map/dot_general | solution.py:43
  52.0 2.5 %convolution_convert_fusion.1 = bf16[384,2560]{1,0:T(8,128)(2,1)} fusion(bf16[320,384]{1,0:T(8,128)(2,1)S(1)} %get-tuple-element.10, bf16[320,2560]{1,0:T(8,128)(2,1)S(1)} %bitcast.42), kind=kOutput, calls=%fused_computation.2 | convolution fusion | flops 630128640 | bytes 3850240 | tf_op jit(solution)/shard_map/dot_general | solution.py:52
  54.5 2.5 %convolution_convert_fusion = bf16[384,2560]{1,0:T(8,128)(2,1)} fusion(bf16[320,384]{1,0:T(8,128)(2,1)S(1)} %get-tuple-element.12, bf16[320,2560]{1,0:T(8,128)(2,1)S(1)} %bitcast.43), kind=kOutput, calls=%fused_computation.1 | convolution fusion | flops 630128640 | bytes 3850240 | tf_op jit(solution)/shard_map/dot_general | solution.py:55
  57.0 0.0 all-reduce.3.cloned.1.call-update
  57.0 0.0 reduce-scatter.2.cloned.1.call-start
  57.0 2.6 %fusion.6 = f32[320,2560]{1,0:T(8,128)S(1)} fusion(bf16[320,384]{1,0:T(8,128)(2,1)S(1)} %get-tuple-element.10, bf16[1,384,2560]{2,1,0:T(8,128)(2,1)} %param.7), kind=kOutput, calls=%fused_computation.13 | convolution fusion | flops 629145600 | bytes 5488640 | tf_op jit(solution)/shard_map/dot_general | solution.py:68
  59.6 1.0 fusion
  60.6 47.2 %all_to_all.5 = bf16[4,80,2560]{2,1,0:T(8,128)(2,1)S(1)} all-to-all(bf16[4,80,2560]{2,1,0:T(8,128)(2,1)S(1)} %bitcast.37), channel_id=1, replica_groups=mesh['rep'=4,'shard'=2,'exp'=4] {'exp'}, dimensions={0} | all-to-all | bytes 3276800 | tf_op jit(solution)/shard_map/all_to_all | solution.py:73
  107.8 1.4 convolution_convert_fusion.3
  109.2 0.0 reduce-scatter.2.cloned.1.call-update
  109.2 55.0 %all-reduce.3.cloned.1.call-done = (bf16[384,2560]{1,0:T(8,128)(2,1)}, bf16[384,2560]{1,0:T(8,128)(2,1)}) async-done(((bf16[384,2560]{1,0:T(8,128)(2,1)}, bf16[384,2560]{1,0:T(8,128)(2,1)}), (bf16[384,2560]{1,0:T(8,128)(2,1)}, bf16[384,2560]{1,0:T(8,128)(2,1)})) %all-reduce.3.cloned.1.call-update) | async-done | bytes 3932176 | tf_op jit(solution)/shard_map/psum | solution.py:59
  164.2 4.7 %fusion.1 = (bf16[1,384,2560]{2,1,0:T(8,128)(2,1)}, bf16[1,384,2560]{2,1,0:T(8,128)(2,1)}) fusion(bf16[384,2560]{1,0:T(8,128)(2,1)} %get-tuple-element.4, bf16[384,2560]{1,0:T(8,128)(2,1)} %get-tuple-element.5), kind=kLoop, calls=%fused_computation.8 | loop fusion | flops 5898240 | bytes 7864320 | tf_op jit(solution)/shard_map/broadcast_in_dim | solution.py:66
  169.0 0.0 reduce-scatter.2.cloned.1.call-done
  (3 shorter events, 0.1 us)
Async XLA Ops:
  8.0 42.1 %copy-start = (bf16[1,384,2560]{2,1,0:T(8,128)(2,1)S(1)}, bf16[1,384,2560]{2,1,0:T(8,128)(2,1)}, u32[]{:S(2)}) copy-start(bf16[1,384,2560]{2,1,0:T(8,128)(2,1)} %param.8) | copy-start | bytes 5898244
  8.0 156.2 %all-reduce.3.cloned.1.call-start = ((), (), s32[]{:S(2)}) async-start(), calls=%async_computation.3 | async-start | bytes 7864320 | tf_op jit(solution)/shard_map/psum | solution.py:59
  13.4 1.4 copy-start.1
  15.0 34.0 %copy-start.2 = (bf16[1,384,2560]{2,1,0:T(8,128)(2,1)S(1)}, bf16[1,384,2560]{2,1,0:T(8,128)(2,1)}, u32[]{:S(2)}) copy-start(bf16[1,384,2560]{2,1,0:T(8,128)(2,1)} %param.7) | copy-start | bytes 5898244
  15.0 20.6 %collective-permute-start = (bf16[1,80,2560]{2,1,0:T(8,128)(2,1)S(1)}, bf16[1,80,2560]{2,1,0:T(8,128)(2,1)S(1)}, u32[]{:S(2)}, u32[]{:S(2)}) collective-permute-start(bf16[1,80,2560]{2,1,0:T(8,128)(2,1)S(1)} %get-tuple-element.8), channel_id=1, source_target_pairs={{0,1},{1,0},{2,3},{3,2},{4,5},{5,4},{6,7},{7,6},{8,9},{9,8},{10,11... | collective-permute-start | bytes 1228808 | tf_op jit(solution)/shard_map/ppermute | solution.py:34
  18.1 30.8 %collective-permute-start.1 = (bf16[1,80,2560]{2,1,0:T(8,128)(2,1)S(1)}, bf16[1,80,2560]{2,1,0:T(8,128)(2,1)S(1)}, u32[]{:S(2)}, u32[]{:S(2)}) collective-permute-start(bf16[1,80,2560]{2,1,0:T(8,128)(2,1)S(1)} %get-tuple-element.7), channel_id=1, source_target_pairs={{0,2},{1,3},{2,0},{3,1},{4,6},{5,7},{6,4},{7,5},{8,10},{9,11},{10,... | collective-permute-start | bytes 1228808 | tf_op jit(solution)/shard_map/ppermute | solution.py:34
  20.7 28.3 %collective-permute-start.2 = (bf16[1,80,2560]{2,1,0:T(8,128)(2,1)S(1)}, bf16[1,80,2560]{2,1,0:T(8,128)(2,1)S(1)}, u32[]{:S(2)}, u32[]{:S(2)}) collective-permute-start(bf16[1,80,2560]{2,1,0:T(8,128)(2,1)S(1)} %get-tuple-element.6), channel_id=1, source_target_pairs={{0,3},{1,2},{2,1},{3,0},{4,7},{5,6},{6,5},{7,4},{8,11},{9,10},{10,... | collective-permute-start | bytes 1228808 | tf_op jit(solution)/shard_map/ppermute | solution.py:34
  49.0 1.1 copy-start.3
  57.0 112.0 %reduce-scatter.2.cloned.1.call-start = ((), (), s32[]{:S(2)}) async-start(), calls=%async_computation.2 | async-start | bytes 983040 | tf_op jit(solution)/shard_map/reduce_scatter | solution.py:80
Sparse Core Ops, SparseCore 0:
  57.1 107.0 all-reduce.2
Sparse Core Ops, SparseCore 1:
  109.3 7.1 reduce-scatter.1
